TPU v7x, 32 devices: a whole 2x2x4 slice. The times are simulated.
32 devices in a mesh: shot: 8 (over y, x, core), depth: 4 (over z).
Axes of the slice: x: 2, y: 2, z: 4, core: 2. Of those that a mesh axis runs over, the one named last changes fastest.
Arguments:
- probes: bfloat16 [8, 64, 128, 128], P('shot', None, 'depth'), may hold values from -6 to 6
- courant: float32 [128, 128], P('depth'), may hold values from 0.1 to 0.45
- sketches: float32 [8, 128, 64], replicated, may hold values from -0.5 to 0.5
Outputs:
- basis: float32 [64, 128, 128], P(None, 'depth')
- cores: float32 [8, 64, 64], P('shot')
All inputs are finite; a program needn't handle non-finite values.
Results may differ from a plain program's by a relative error of at most 0.0003.
Values may be sent and summed in bfloat16 or wider, within the bound.
A program may use at most 64 MiB of HBM per device.

v0:
```python
import functools
import math

import jax
import jax.numpy as jnp
from jax import lax
from jax.experimental import pallas as pl
from jax.experimental.pallas import tpu as pltpu
from jax.sharding import PartitionSpec as P

STEPS = 4
MESH = pl.DeviceIdType.MESH
HI = lax.Precision.HIGHEST
NN = (((1,), (0,)), ((), ()))
NT = (((1,), (1,)), ((), ()))
TN = (((0,), (0,)), ((), ()))
PIECES = 2
WIDTH = 8


def mm(a, b, dims=NN):
    return lax.dot_general(a, b, dims, precision=HI, preferred_element_type=jnp.float32)


def split(x):
    top = x.astype(jnp.bfloat16)
    return top, (x - top.astype(jnp.float32)).astype(jnp.bfloat16)


def mm3(a, b, dims=NN):
    def part(p, q):
        return lax.dot_general(p, q, dims, preferred_element_type=jnp.float32)

    return part(a[0], b[0]) + (part(a[0], b[1]) + part(a[1], b[0]))


def wide(ref, h, d, picked=slice(None)):
    return jnp.concatenate([ref[h, d + i, picked] for i in range(WIDTH)], axis=1)


def inverse_factor(gram):
    n = gram.shape[0]
    rows = lax.broadcasted_iota(jnp.int32, (n, 1), 0)
    eye = (
        lax.broadcasted_iota(jnp.int32, (n, n), 0) == lax.broadcasted_iota(jnp.int32, (n, n), 1)
    ).astype(jnp.float32)
    a = jnp.concatenate([gram, eye], axis=1)
    blocks = [a[8 * b : 8 * b + 8] for b in range(n // 8)]
    for k in range(0, n, 2):
        b0, r = divmod(k, 8)
        first, second = blocks[b0][r : r + 1], blocks[b0][r + 1 : r + 2]
        p, q, s = first[:, k : k + 1], second[:, k : k + 1], second[:, k + 1 : k + 2]
        if k == n - 2:
            break
        scale = 1.0 / (p * s - q * q)
        row0 = (s * first - q * second) * scale
        row1 = (p * second - q * first) * scale
        for b in range((k + 2) // 8, n // 8):
            col0, col1 = blocks[b][:, k : k + 1], blocks[b][:, k + 1 : k + 2]
            if b == b0:
                below = rows[:8] > r + 1
                col0, col1 = jnp.where(below, col0, 0.0), jnp.where(below, col1, 0.0)
            blocks[b] = blocks[b] - (col0 * row0 + col1 * row1)
    a = jnp.concatenate(blocks, axis=0)
    before = jnp.concatenate([a[n - 1 :], a[: n - 1]], axis=0)
    even = lax.rem(rows, 2) == 0
    own = jnp.sum(a[:, :n] * eye, axis=1, keepdims=True)
    shifted = jnp.concatenate([eye[n - 1 :], eye[: n - 1]], axis=0)
    side = jnp.sum(a[:, :n] * shifted, axis=1, keepdims=True)
    above = jnp.sum(before[:, :n] * shifted, axis=1, keepdims=True)
    ratio = jnp.where(even, 0.0, side / jnp.where(even, 1.0, above))
    value = own - ratio * side
    return (a[:, n:] - ratio * before[:, n:]) * (1.0 / jnp.sqrt(value))


def kernel(
    depths,
    levels,
    probes,
    speed,
    sketches,
    basis,
    cores,
    halo,
    wide_speed,
    field_a,
    field_b,
    pairs,
    sums,
    sums_in,
    halo_send,
    halo_recv,
    speed_send,
    speed_recv,
    pair_send,
    pair_recv,
    sum_send,
    sum_recv,
):
    rows, rank, cells = probes.shape
    shot = lax.axis_index("shot")
    depth = lax.axis_index("depth")
    low_end = depth == 0
    high_end = depth == depths - 1

    def bit(h):
        return lax.rem(shot // (2**h), 2)

    def peer(h):
        return shot + 2**h - 2 ** (h + 1) * bit(h)

    barrier = pltpu.get_barrier_semaphore()
    for h in range(levels):
        pl.semaphore_signal(barrier, inc=1, device_id=(peer(h), depth), device_id_type=MESH)
    for j in range(1, depths):
        other = lax.rem(depth + j, depths)
        pl.semaphore_signal(barrier, inc=1, device_id=(shot, other), device_id_type=MESH)
    pl.semaphore_wait(barrier, levels + depths - 1)

    def halo_copies(side):
        to = depth + 1 if side == 0 else depth - 1
        rows_out = pl.ds(rows - STEPS, STEPS) if side == 0 else pl.ds(0, STEPS)
        first = pltpu.make_async_remote_copy(
            src_ref=probes.at[rows_out],
            dst_ref=halo.at[side],
            send_sem=halo_send.at[side],
            recv_sem=halo_recv.at[side],
            device_id=(shot, to),
            device_id_type=MESH,
        )
        at = 0 if side == 0 else STEPS + rows
        second = pltpu.make_async_remote_copy(
            src_ref=speed.at[rows_out],
            dst_ref=wide_speed.at[pl.ds(at, STEPS)],
            send_sem=speed_send.at[side],
            recv_sem=speed_recv.at[side],
            device_id=(shot, to),
            device_id_type=MESH,
        )
        return first, second

    @pl.when(depth < depths - 1)
    def _():
        for c in halo_copies(0):
            c.start()

    @pl.when(depth > 0)
    def _():
        for c in halo_copies(1):
            c.start()

    @pl.loop(0, rows, unroll=4)
    def _(d):
        field_a[STEPS + d] = probes[d].astype(jnp.float32)

    wide_speed[STEPS : STEPS + rows] = speed[...]

    @pl.when(depth > 0)
    def _():
        for c in halo_copies(0):
            c.wait_recv()
        field_a[0:STEPS] = halo[0].astype(jnp.float32)

    @pl.when(depth == 0)
    def _():
        field_a[0:STEPS] = jnp.zeros((STEPS, rank, cells), jnp.float32)
        wide_speed[0:STEPS] = jnp.zeros((STEPS, cells), jnp.float32)

    @pl.when(depth < depths - 1)
    def _():
        for c in halo_copies(1):
            c.wait_recv()
        field_a[STEPS + rows : 2 * STEPS + rows] = halo[1].astype(jnp.float32)

    @pl.when(depth == depths - 1)
    def _():
        field_a[STEPS + rows : 2 * STEPS + rows] = jnp.zeros((STEPS, rank, cells), jnp.float32)
        wide_speed[STEPS + rows : 2 * STEPS + rows] = jnp.zeros((STEPS, cells), jnp.float32)

    lane = lax.broadcasted_iota(jnp.int32, (rank, cells), 1)
    not_first = lane > 0
    not_last = lane < cells - 1
    me = bit(0)
    mine = pl.ds(pl.multiple_of(me * rank, rank), rank)

    def update(d, source, older):
        u = source[d]
        left = jnp.where(not_first, pltpu.roll(u, 1, 1), 0.0)
        right = jnp.where(not_last, pltpu.roll(u, cells - 1, 1), 0.0)
        laplace = source[d + 1] + source[d - 1] + right + left - 4.0 * u
        return 2.0 * u - older + wide_speed[pl.ds(d, 1)] * laplace

    for step in range(STEPS):
        source, target = (field_a, field_b) if step % 2 == 0 else (field_b, field_a)
        last = step == STEPS - 1

        @pl.loop(step + 1, 2 * STEPS + rows - step - 1, unroll=2)
        def _(d):
            older = source[d] if step == 0 else target[d]
            new = update(d, source, older)
            if last:
                pairs[0, d - STEPS, mine] = new
            else:
                target[d] = new

    def pair_copy(h):
        own = pl.ds(pl.multiple_of(bit(h) * rank, rank), rank)
        return [
            pltpu.make_async_remote_copy(
                src_ref=pairs.at[h, :, own],
                dst_ref=pairs.at[h, :, own],
                send_sem=pair_send.at[h, 0, 0],
                recv_sem=pair_recv.at[h, 0, 0],
                device_id=(peer(h), depth),
                device_id_type=MESH,
            )
        ]

    for c in pair_copy(0):
        c.start()
    for c in pair_copy(0):
        c.wait()

    def gram_body(d, total):
        x = split(wide(pairs, 0, d * WIDTH))
        return total + mm3(x, x, NT)

    zero = jnp.zeros((2 * rank, 2 * rank), jnp.float32)
    gram = lax.fori_loop(0, rows // WIDTH, gram_body, zero)

    def sum_copy(h, j):
        other = lax.rem(depth + j, depths)
        size = 2 * rank if h == 0 else rank
        return pltpu.make_async_remote_copy(
            src_ref=sums.at[h, pl.ds(0, size)],
            dst_ref=sums_in.at[h, depth, pl.ds(0, size)],
            send_sem=sum_send.at[h, j],
            recv_sem=sum_recv.at[h, j],
            device_id=(shot, other),
            device_id_type=MESH,
        )

    def depth_sum(h, value):
        size = value.shape[0]
        sums[h, 0:size] = value
        for j in range(1, depths):
            sum_copy(h, j).start()
        for j in range(1, depths):
            sum_copy(h, j).wait()
        total = None
        for j in range(depths):
            part = jnp.where(depth == j, value, sums_in[h, j, 0:size])
            total = part if total is None else total + part
        return total

    for h in range(levels):
        sums_in[h, depth] = jnp.zeros((2 * rank, 2 * rank), jnp.float32)
    gram = depth_sum(0, gram)

    low = inverse_factor(gram[:rank, :rank])
    high = inverse_factor(gram[rank:, rank:])
    sketch = sketches[shot // 2 * 2]
    mixer = jnp.concatenate(
        [mm(sketch[:rank], low, TN), mm(sketch[rank:], high, TN)], axis=1
    )
    carried = mm(mixer, gram)
    inverse = inverse_factor(mm(carried, mixer, NT))
    mixer = mm(inverse, mixer)
    carried = mm(inverse, carried)
    projected = jnp.where(me == 0, carried[:, :rank], carried[:, rank:])

    for h in range(1, levels):
        own_bit = bit(h)
        own = pl.ds(pl.multiple_of(own_bit * rank, rank), rank)

        parts = split(mixer)
        part_rows = rows // 2**h
        per = part_rows // PIECES
        got = pl.ds(pl.multiple_of((1 - own_bit) * rank, rank), rank)

        def part_at(mask, i):
            part = 0
            for b in range(h):
                part += 2**b * (1 - bit(b) if mask >> b & 1 else bit(b))
            return pl.ds(part * part_rows + i * per, per)

        def part_copy(mask, i):
            low = mask & -mask
            at = part_at(mask - low, i)
            lanes = got if mask else own
            return pltpu.make_async_remote_copy(
                src_ref=pairs.at[h, at, lanes],
                dst_ref=pairs.at[h, at, lanes],
                send_sem=pair_send.at[h, mask, i],
                recv_sem=pair_recv.at[h, mask, i],
                device_id=(peer(low.bit_length() - 1 if mask else h), depth),
                device_id_type=MESH,
            )

        chunks = rows // WIDTH
        ahead = max(1, part_rows // WIDTH)
        first = part_at(0, 0).start // WIDTH
        for t in range(chunks):
            at = lax.rem(first + t, chunks) * WIDTH
            out = mm3(parts, split(wide(pairs, h - 1, at)))
            for w in range(WIDTH):
                pairs[h, at + w, own] = out[:, w * cells : (w + 1) * cells]
            if per == WIDTH and t < PIECES:
                part_copy(0, t).start()
            elif per != WIDTH and t == ahead - 1:
                for i in range(PIECES):
                    part_copy(0, i).start()
        masks = sorted(range(2**h), key=lambda m: (m.bit_count(), -m))
        for mask in masks:
            low = mask & -mask if mask else 2**h
            for i in range(PIECES):
                part_copy(mask, i).wait_recv()
                for b in reversed(range(low.bit_length() - 1)):
                    part_copy(mask + 2**b, i).start()
        for mask in masks:
            for i in range(PIECES):
                part_copy(mask, i).wait_send()

        def cross_body(d, total):
            y = split(wide(pairs, h, d * WIDTH))
            r = split(wide(pairs, 0, d * WIDTH, mine))
            right = [jnp.concatenate([p[rank:], q], axis=0) for p, q in zip(y, r)]
            return total + mm3(y, right, NT)

        cross = lax.fori_loop(0, rows // WIDTH, cross_body, zero)
        value = jnp.concatenate(
            [
                cross[:rank, :rank],
                jnp.where(own_bit == 0, cross[rank:, rank:], cross[:rank, rank:]),
            ],
            axis=1,
        )
        value = depth_sum(h, value)
        stride = 2**h
        sketch = sketches[shot // (2 * stride) * (2 * stride) + stride - 1]
        top, bottom = sketch[:rank], sketch[rank:]
        across = value[:, :rank]
        mixed = mm(sketch, sketch, TN)
        mixed += mm(top, mm(across, bottom), TN) + mm(bottom, mm(across, top, TN), TN)
        inverse = inverse_factor(mixed)
        mixer = mm(inverse, sketch, NT)
        other = value[:, rank:]
        low_part = jnp.where(own_bit == 0, projected, other)
        high_part = jnp.where(own_bit == 0, other, projected)
        projected = mm(mixer, jnp.concatenate([low_part, high_part], axis=0))

    parts = split(mixer)

    @pl.loop(0, rows // WIDTH)
    def _(i):
        out = mm3(parts, split(wide(pairs, levels - 1, i * WIDTH)))
        for w in range(WIDTH):
            basis[i * WIDTH + w] = out[:, w * cells : (w + 1) * cells]

    cores[...] = projected * (1.0 / math.sqrt(rank))

    @pl.when(depth < depths - 1)
    def _():
        for c in halo_copies(0):
            c.wait_send()

    @pl.when(depth > 0)
    def _():
        for c in halo_copies(1):
            c.wait_send()


def body(probes, courant, sketches):
    depths = lax.axis_size("depth")
    levels = lax.axis_size("shot").bit_length() - 1
    local = jnp.transpose(probes[0], (1, 0, 2))
    rows, rank, cells = local.shape
    f32 = jnp.float32
    vmem = pl.BlockSpec(memory_space=pltpu.VMEM)
    dma = pltpu.SemaphoreType.DMA
    basis, cores = pl.pallas_call(
        functools.partial(kernel, depths, levels),
        out_shape=(
            jax.ShapeDtypeStruct((rows, rank, cells), f32),
            jax.ShapeDtypeStruct((rank, rank), f32),
        ),
        in_specs=[vmem] * 3,
        out_specs=(vmem, vmem),
        scratch_shapes=[
            pltpu.VMEM((2, STEPS, rank, cells), jnp.bfloat16),
            pltpu.VMEM((rows + 2 * STEPS, cells), f32),
            pltpu.VMEM((rows + 2 * STEPS, rank, cells), f32),
            pltpu.VMEM((rows + 2 * STEPS, rank, cells), f32),
            pltpu.VMEM((levels, rows, 2 * rank, cells), f32),
            pltpu.VMEM((levels, 2 * rank, 2 * rank), f32),
            pltpu.VMEM((levels, depths, 2 * rank, 2 * rank), f32),
            dma((2,)),
            dma((2,)),
            dma((2,)),
            dma((2,)),
            dma((levels, 2 ** (levels - 1), PIECES)),
            dma((levels, 2 ** (levels - 1), PIECES)),
            dma((levels, depths)),
            dma((levels, depths)),
        ],
        compiler_params=pltpu.CompilerParams(
            collective_id=0, has_side_effects=True, vmem_limit_bytes=56 * 2**20
        ),
    )(local, courant, sketches)
    return (jnp.transpose(basis, (1, 0, 2)), cores[None])


def solution(mesh):
    placed = (P("shot", None, "depth", None), P("depth", None), P())
    return jax.shard_map(
        body,
        mesh=mesh,
        in_specs=placed,
        out_specs=(P(None, "depth", None), P("shot", None, None)),
        check_vma=False,
    )
```

profile of v0, /device:TPU:1, one launch (start us, length us, event | category | flops | bytes accessed | tf_op | source)
XLA Modules:
  0.0 101.1 jit_solution(2639954477550345337)
XLA Ops:
  0.6 0.0 copy-start
  0.6 2.1 %copy.9 = bf16[1,64,32,128]{3,1,2,0:T(8,128)(2,1)} copy(bf16[1,64,32,128]{3,2,1,0:T(8,128)(2,1)} %param.3) | data formatting | bytes 1048576 | tf_op args[0]
  2.7 0.0 copy-done
  2.7 1.0 copy.6.sketches
  3.7 93.9 %shard_map.50 = (f32[32,64,128]{2,1,0:T(8,128)}, f32[64,64]{1,0:T(8,128)}) custom-call(bf16[32,64,128]{2,1,0:T(8,128)(2,1)} %bitcast.7, f32[32,128]{1,0:T(8,128)} %speed.1, f32[8,128,64]{2,1,0:T(8,128)} %copy.6.sketches), custom_call_target="tpu_custom_call" | custom-call | tf_op jit(solution)/shard_map/pallas_call | solution.py:381
  97.6 0.0 copy-start.1
  97.7 2.8 %copy.7 = f32[64,32,128]{2,1,0:T(8,128)} copy(f32[64,32,128]{2,0,1:T(8,128)} %bitcast.8) | data formatting | bytes 2097152
  100.5 0.0 copy-done.1
  100.5 0.6 copy.11
Async XLA Ops:
  0.6 2.1 %copy-start = (f32[8,128,64]{1,2,0:T(8,128)S(1)}, f32[8,128,64]{1,2,0:T(8,128)}, u32[]{:S(2)}) copy-start(f32[8,128,64]{1,2,0:T(8,128)} %param.5) | copy-start | bytes 786436
  97.6 2.8 %copy-start.1 = (f32[64,64]{1,0:T(8,128)S(1)}, f32[64,64]{1,0:T(8,128)}, u32[]{:S(2)}) copy-start(f32[64,64]{1,0:T(8,128)} %get-tuple-element.5) | copy-start | bytes 49156
where the time goes:
time: 102 us; the launch traced here: 101 us
  Pallas kernels  93.9 us (92%)
  local copies, waits for them, and re-layouts  6.52 us (6%)
    pallas_call x1, Pallas kernels, body(): pl.pallas_call(functools.partial(kernel, depths, levels), out_shape=(jax....  93.9 us
    unnamed x8, local copies, waits for them, and re-layouts  6.52 us

commit v1 on v0

--- a/solution.py
+++ b/solution.py
@@ -410,10 +410,502 @@
     return (jnp.transpose(basis, (1, 0, 2)), cores[None])
 
 
+def choose(bit_value, low, high):
+    return jnp.where(bit_value == 0, low, high)
+
+
+def merged(sketch, near, theirs):
+    half = mm(
+        jnp.concatenate([0.5 * sketch, near], axis=1),
+        jnp.concatenate([sketch, theirs], axis=1),
+        NT,
+    )
+    return half + jnp.transpose(half)
+
+
+def plane_kernel(
+    depths,
+    probes,
+    speed,
+    sketches,
+    basis,
+    cores,
+    halo,
+    wide_speed,
+    field_a,
+    field_b,
+    pair,
+    whole,
+    first_sum,
+    first_in,
+    gram_all,
+    quad_part,
+    quad_in,
+    quad_sum,
+    quad_depth,
+    quad_all,
+    root_part,
+    root_in,
+    root_sum,
+    root_depth,
+    root_all,
+    quad_mixer,
+    quad_mixer_in,
+    root_mixer,
+    root_mixer_in,
+    gathered,
+    send_sems,
+    recv_sems,
+    local_sems,
+):
+    rows, rank, cells = probes.shape
+    shots = 8
+    per = rows // shots
+    part = 2 * rank // 4
+    shot = lax.axis_index("shot")
+    depth = lax.axis_index("depth")
+
+    def bit(h, of=shot):
+        return lax.rem(of // (2**h), 2)
+
+    def flip(mask, of=shot):
+        value = 0
+        for h in range(3):
+            value += 2**h * (1 - bit(h, of) if mask >> h & 1 else bit(h, of))
+        return value
+
+    core, low_x, low_y = bit(0), bit(1), bit(2)
+
+    barrier = pltpu.get_barrier_semaphore()
+    for mask in range(1, shots):
+        pl.semaphore_signal(barrier, inc=1, device_id=(flip(mask), depth), device_id_type=MESH)
+    for j in range(1, depths):
+        other = lax.rem(depth + j, depths)
+        pl.semaphore_signal(barrier, inc=1, device_id=(shot, other), device_id_type=MESH)
+    pl.semaphore_wait(barrier, shots - 1 + depths - 1)
+
+    used = [0]
+
+    def take(count):
+        used[0] += count
+        return used[0] - count
+
+    def copy(src, dst, sem, to):
+        return pltpu.make_async_remote_copy(
+            src_ref=src,
+            dst_ref=dst,
+            send_sem=send_sems.at[sem],
+            recv_sem=recv_sems.at[sem],
+            device_id=to,
+            device_id_type=MESH,
+        )
+
+    halo_sem, speed_sem = take(2), take(2)
+
+    def halo_copies(side):
+        to = depth + 1 if side == 0 else depth - 1
+        rows_out = pl.ds(rows - STEPS, STEPS) if side == 0 else pl.ds(0, STEPS)
+        at = 0 if side == 0 else STEPS + rows
+        return (
+            copy(probes.at[rows_out], halo.at[side], halo_sem + side, (shot, to)),
+            copy(
+                speed.at[rows_out],
+                wide_speed.at[pl.ds(at, STEPS)],
+                speed_sem + side,
+                (shot, to),
+            ),
+        )
+
+    @pl.when(depth < depths - 1)
+    def _():
+        for c in halo_copies(0):
+            c.start()
+
+    @pl.when(depth > 0)
+    def _():
+        for c in halo_copies(1):
+            c.start()
+
+    @pl.loop(0, rows, unroll=4)
+    def _(d):
+        field_a[STEPS + d] = probes[d].astype(jnp.float32)
+
+    wide_speed[STEPS : STEPS + rows] = speed[...]
+
+    @pl.when(depth > 0)
+    def _():
+        for c in halo_copies(0):
+            c.wait_recv()
+        field_a[0:STEPS] = halo[0].astype(jnp.float32)
+
+    @pl.when(depth == 0)
+    def _():
+        field_a[0:STEPS] = jnp.zeros((STEPS, rank, cells), jnp.float32)
+        wide_speed[0:STEPS] = jnp.zeros((STEPS, cells), jnp.float32)
+
+    @pl.when(depth < depths - 1)
+    def _():
+        for c in halo_copies(1):
+            c.wait_recv()
+        field_a[STEPS + rows : 2 * STEPS + rows] = halo[1].astype(jnp.float32)
+
+    @pl.when(depth == depths - 1)
+    def _():
+        field_a[STEPS + rows : 2 * STEPS + rows] = jnp.zeros((STEPS, rank, cells), jnp.float32)
+        wide_speed[STEPS + rows : 2 * STEPS + rows] = jnp.zeros((STEPS, cells), jnp.float32)
+
+    lane = lax.broadcasted_iota(jnp.int32, (rank, cells), 1)
+    not_first = lane > 0
+    not_last = lane < cells - 1
+    mine = pl.ds(pl.multiple_of(core * rank, rank), rank)
+
+    def update(d, source, older):
+        u = source[d]
+        left = jnp.where(not_first, pltpu.roll(u, 1, 1), 0.0)
+        right = jnp.where(not_last, pltpu.roll(u, cells - 1, 1), 0.0)
+        laplace = source[d + 1] + source[d - 1] + right + left - 4.0 * u
+        return 2.0 * u - older + wide_speed[pl.ds(d, 1)] * laplace
+
+    for step in range(STEPS - 1):
+        source, target = (field_a, field_b) if step % 2 == 0 else (field_b, field_a)
+
+        @pl.loop(step + 1, 2 * STEPS + rows - step - 1, unroll=2)
+        def _(d):
+            older = source[d] if step == 0 else target[d]
+            target[d] = update(d, source, older)
+
+    pair_sem, spread_sem = take(shots), take(shots)
+
+    def pair_copy(i):
+        at = pl.ds(i * per, per)
+        return copy(pair.at[at, mine], pair.at[at, mine], pair_sem + i, (flip(1), depth))
+
+    def spread_copy(to, mask):
+        at = pl.ds(to * per, per)
+        into = pl.ds(pl.multiple_of(shot * rank, rank), rank)
+        return copy(pair.at[at, mine], whole.at[:, into], spread_sem + mask, (to, depth))
+
+    source, target = (field_a, field_b) if (STEPS - 1) % 2 == 0 else (field_b, field_a)
+
+    @pl.loop(0, shots)
+    def _(i):
+        for w in range(per):
+            d = STEPS + i * per + w
+            pair[i * per + w, mine] = update(d, source, target[d])
+        pair_copy(i).start()
+
+        @pl.when(i // 2 != shot // 2)
+        def _():
+            mask = 0
+            for h in range(3):
+                mask += 2**h * lax.rem(bit(h, i) + bit(h), 2)
+            spread_copy(i, mask).start()
+
+    group = WIDTH // per
+
+    def gram_body(t, total):
+        for i in range(group):
+            pair_copy(t * group + i).wait_recv()
+        at = t * WIDTH
+        x = split(jnp.concatenate([pair[at + i] for i in range(WIDTH)], axis=1))
+        return total + mm3(x, x, NT)
+
+    zero = jnp.zeros((2 * rank, 2 * rank), jnp.float32)
+    gram = lax.fori_loop(0, rows // WIDTH, gram_body, zero)
+
+    def depth_start(source, into, sem):
+        for j in range(1, depths):
+            other = lax.rem(depth + j, depths)
+            copy(source, into.at[depth], sem + j, (shot, other)).start()
+
+    def depth_finish(source, into, sem, value):
+        for j in range(1, depths):
+            other = lax.rem(depth + j, depths)
+            copy(source, into.at[depth], sem + j, (shot, other)).wait_recv()
+        total = None
+        for j in range(depths):
+            one = jnp.where(depth == j, value, into[j])
+            total = one if total is None else total + one
+        return total
+
+    for into in (first_in, quad_depth, root_depth):
+        into[depth] = jnp.zeros(into.shape[1:], jnp.float32)
+
+    first_sem, first_pair_sem = take(depths), take(1)
+    half = choose(core, gram[:rank], gram[rank:])
+    first_sum[...] = half
+    depth_start(first_sum, first_in, first_sem)
+    own_rows = pl.ds(pl.multiple_of(shot // 2 * 2 * rank, 2 * rank), 2 * rank)
+    for w in range(per):
+        whole[w, own_rows] = pair[shot * per + w]
+    gram_all[mine] = depth_finish(first_sum, first_in, first_sem, half)
+    first_pair = copy(gram_all.at[mine], gram_all.at[mine], first_pair_sem, (flip(1), depth))
+    first_pair.start()
+    first_pair.wait_recv()
+    gram = gram_all[...]
+
+    low = inverse_factor(gram[:rank, :rank])
+    high = inverse_factor(gram[rank:, rank:])
+
+    for mask in range(2, shots):
+        spread_copy(flip(mask), mask).wait_recv()
+
+    def cross(first, second, size):
+        total = None
+        for w in range(0, per, 2):
+            x = split(jnp.concatenate([whole[w, first : first + size], whole[w + 1, first : first + size]], axis=1))
+            y = split(jnp.concatenate([whole[w, second : second + size], whole[w + 1, second : second + size]], axis=1))
+            one = mm3(x, y, NT)
+            total = one if total is None else total + one
+        return total
+
+    quad_sem, quad_depth_sem, quad_all_sem = take(shots), take(depths), take(4)
+    root_sem, root_depth_sem, root_all_sem = take(shots), take(depths), take(shots)
+    tall = 2 * rank // 4
+    for q in range(2):
+        value = cross(4 * rank * q, 4 * rank * q + 2 * rank, 2 * rank)
+        for i in range(4):
+            quad_part[4 * q + i] = value[i * tall : (i + 1) * tall]
+
+    def scatter(source, into, sem, mask):
+        return copy(source.at[flip(mask)], into.at[mask], sem + mask, (flip(mask), depth))
+
+    for mask in range(1, shots):
+        scatter(quad_part, quad_in, quad_sem, mask).start()
+    value = cross(0, 4 * rank, 4 * rank)
+    for i in range(shots):
+        root_part[i] = value[i * tall : (i + 1) * tall]
+    for mask in range(1, shots):
+        scatter(root_part, root_in, root_sem, mask).start()
+
+    def scattered(source, into, sem):
+        total = source[shot]
+        for mask in range(1, shots):
+            scatter(source, into, sem, mask).wait_recv()
+            total = total + into[mask]
+        return total
+
+    def piece_copy(ref, at, sem, mask):
+        here = pl.ds(pl.multiple_of(at * tall, tall), tall)
+        return copy(ref.at[here], ref.at[here], sem + mask, (flip(mask), depth))
+
+    sketch = sketches[shot // 2 * 2]
+    left = mm(sketch[:, :rank], low)
+    right = mm(sketch[:, rank:], high)
+    mixed = merged(sketch, mm(left, gram[:rank, rank:]), right)
+
+    quad_own = scattered(quad_part, quad_in, quad_sem)
+    quad_sum[...] = quad_own
+    depth_start(quad_sum, quad_depth, quad_depth_sem)
+
+    inverse = inverse_factor(mixed)
+    sketch = sketches[shot // 4 * 4 + 1]
+    carry = mm(choose(low_x, sketch[:, :rank], sketch[:, rank:]), inverse)
+    mine_quad = mm(carry, jnp.concatenate([left, right], axis=1))
+    quad_mixer[...] = mine_quad
+    exchange_sem = take(2)
+    quad_exchange = copy(quad_mixer, quad_mixer_in, exchange_sem, (flip(2), depth))
+    quad_exchange.start()
+
+    quad_at = 2 * low_x + core
+    quad_all[pl.ds(pl.multiple_of(quad_at * tall, tall), tall)] = depth_finish(
+        quad_sum, quad_depth, quad_depth_sem, quad_own
+    )
+    for mask in range(1, 4):
+        piece_copy(quad_all, quad_at, quad_all_sem, mask).start()
+    root_own = scattered(root_part, root_in, root_sem)
+    root_sum[...] = root_own
+    depth_start(root_sum, root_depth, root_depth_sem)
+    for mask in range(1, 4):
+        piece_copy(quad_all, quad_at, quad_all_sem, mask).wait_recv()
+
+    quad = quad_all[...]
+    near = choose(low_x, mm(mine_quad, quad), mm(mine_quad, quad, NT))
+    quad_exchange.wait_recv()
+    their_quad = quad_mixer_in[...]
+    mixed = merged(sketch, near, their_quad)
+
+    root_all[pl.ds(pl.multiple_of(shot * tall, tall), tall)] = depth_finish(
+        root_sum, root_depth, root_depth_sem, root_own
+    )
+    for mask in range(1, shots):
+        piece_copy(root_all, shot, root_all_sem, mask).start()
+
+    inverse = inverse_factor(mixed)
+    sketch = sketches[3]
+    carry = mm(choose(low_y, sketch[:, :rank], sketch[:, rank:]), inverse)
+    joined = jnp.concatenate(
+        [
+            choose(low_x, mine_quad, their_quad),
+            choose(low_x, their_quad, mine_quad),
+        ],
+        axis=1,
+    )
+    mine_root = mm(carry, joined)
+    root_mixer[...] = mine_root
+    root_exchange = copy(root_mixer, root_mixer_in, exchange_sem + 1, (flip(4), depth))
+    root_exchange.start()
+    for mask in range(1, shots):
+        piece_copy(root_all, shot, root_all_sem, mask).wait_recv()
+
+    root = root_all[...]
+    near = choose(low_y, mm(mine_root, root), mm(mine_root, root, NT))
+    root_exchange.wait_recv()
+    their_root = root_mixer_in[...]
+    inverse = inverse_factor(merged(sketch, near, their_root))
+    mine_root = mm(inverse, mine_root)
+    their_root = mm(inverse, their_root)
+    mixer = jnp.concatenate(
+        [
+            choose(low_y, mine_root, their_root),
+            choose(low_y, their_root, mine_root),
+        ],
+        axis=1,
+    )
+
+    share_sem = take(2 * shots)
+    parts = split(mixer)
+
+    def share_copy(mask, i):
+        at = pl.ds(shot * per + 2 * i, 2)
+        return copy(gathered.at[at], gathered.at[at], share_sem + 2 * mask + i, (flip(mask), depth))
+
+    def forward_copy(mask, i):
+        at = pl.ds(flip(mask) * per + 2 * i, 2)
+        return copy(gathered.at[at], gathered.at[at], share_sem + 2 * (mask + 1) + i, (flip(1), depth))
+
+    for i in range(per // 2):
+        out = mm3(parts, split(jnp.concatenate([whole[2 * i], whole[2 * i + 1]], axis=1)))
+        for w in range(2):
+            gathered[shot * per + 2 * i + w] = out[:, w * cells : (w + 1) * cells]
+        for mask in (6, 2, 4, 1):
+            share_copy(mask, i).start()
+
+    own = choose(low_x, mine_root[:, : 2 * rank], mine_root[:, 2 * rank :])
+    other = choose(low_x, mine_root[:, 2 * rank :], mine_root[:, : 2 * rank])
+    near = mm(own, gram)
+    near += choose(low_x, mm(other, quad, NT), mm(other, quad))
+    far = choose(low_y, mm(their_root, root, NT), mm(their_root, root))
+    near += choose(low_x, far[:, : 2 * rank], far[:, 2 * rank :])
+    cores[...] = choose(core, near[:, :rank], near[:, rank:]) * (1.0 / math.sqrt(rank))
+
+    for i in range(per // 2):
+        for mask in (2, 4, 6):
+            share_copy(mask, i).wait_recv()
+            forward_copy(mask, i).start()
+    for i in range(per // 2):
+        for mask in (1, 3, 5, 7):
+            share_copy(mask, i).wait_recv()
+
+    out_copy = pltpu.make_async_copy(gathered, basis, local_sems.at[0])
+    out_copy.start()
+
+    @pl.when(depth < depths - 1)
+    def _():
+        for c in halo_copies(0):
+            c.wait_send()
+
+    @pl.when(depth > 0)
+    def _():
+        for c in halo_copies(1):
+            c.wait_send()
+
+    for i in range(shots):
+        pair_copy(i).wait_send()
+    for mask in range(2, shots):
+        spread_copy(flip(mask), mask).wait_send()
+    for source, into, sem in (
+        (first_sum, first_in, first_sem),
+        (quad_sum, quad_depth, quad_depth_sem),
+        (root_sum, root_depth, root_depth_sem),
+    ):
+        for j in range(1, depths):
+            other = lax.rem(depth + j, depths)
+            copy(source, into.at[depth], sem + j, (shot, other)).wait_send()
+    first_pair.wait_send()
+    for mask in range(1, shots):
+        scatter(quad_part, quad_in, quad_sem, mask).wait_send()
+        scatter(root_part, root_in, root_sem, mask).wait_send()
+        piece_copy(root_all, shot, root_all_sem, mask).wait_send()
+    for mask in range(1, 4):
+        piece_copy(quad_all, quad_at, quad_all_sem, mask).wait_send()
+    quad_exchange.wait_send()
+    root_exchange.wait_send()
+    for i in range(per // 2):
+        for mask in (1, 2, 4, 6):
+            share_copy(mask, i).wait_send()
+        for mask in (2, 4, 6):
+            forward_copy(mask, i).wait_send()
+    out_copy.wait()
+    assert used[0] <= SEMS
+
+
+SEMS = 112
+
+
+def plane_body(probes, courant, sketches):
+    depths = lax.axis_size("depth")
+    shots = lax.axis_size("shot")
+    local = jnp.transpose(probes[0], (1, 0, 2))
+    rows, rank, cells = local.shape
+    per = rows // shots
+    tall = rank // 2
+    f32 = jnp.float32
+    vmem = pl.BlockSpec(memory_space=pltpu.VMEM)
+    dma = pltpu.SemaphoreType.DMA
+
+    def scratch(*shape):
+        return pltpu.VMEM(shape, f32)
+
+    basis, cores = pl.pallas_call(
+        functools.partial(plane_kernel, depths),
+        out_shape=(
+            jax.ShapeDtypeStruct((rows, rank, cells), f32),
+            jax.ShapeDtypeStruct((rank, rank), f32),
+        ),
+        in_specs=[vmem] * 3,
+        out_specs=(pl.BlockSpec(memory_space=pl.ANY), vmem),
+        scratch_shapes=[
+            pltpu.VMEM((2, STEPS, rank, cells), jnp.bfloat16),
+            scratch(rows + 2 * STEPS, cells),
+            scratch(rows + 2 * STEPS, rank, cells),
+            scratch(rows + 2 * STEPS, rank, cells),
+            scratch(rows, 2 * rank, cells),
+            scratch(per, shots * rank, cells),
+            scratch(rank, 2 * rank),
+            scratch(depths, rank, 2 * rank),
+            scratch(2 * rank, 2 * rank),
+            scratch(shots, tall, 2 * rank),
+            scratch(shots, tall, 2 * rank),
+            scratch(tall, 2 * rank),
+            scratch(depths, tall, 2 * rank),
+            scratch(2 * rank, 2 * rank),
+            scratch(shots, tall, 4 * rank),
+            scratch(shots, tall, 4 * rank),
+            scratch(tall, 4 * rank),
+            scratch(depths, tall, 4 * rank),
+            scratch(4 * rank, 4 * rank),
+            scratch(rank, 2 * rank),
+            scratch(rank, 2 * rank),
+            scratch(rank, 4 * rank),
+            scratch(rank, 4 * rank),
+            scratch(rows, rank, cells),
+            dma((SEMS,)),
+            dma((SEMS,)),
+            dma((1,)),
+        ],
+        compiler_params=pltpu.CompilerParams(
+            collective_id=0, has_side_effects=True, vmem_limit_bytes=56 * 2**20
+        ),
+    )(local, courant, jnp.transpose(sketches, (0, 2, 1)))
+    return (jnp.transpose(basis, (1, 0, 2)), cores[None])
+
+
 def solution(mesh):
     placed = (P("shot", None, "depth", None), P("depth", None), P())
+    plane = mesh.shape["shot"] == 8
     return jax.shard_map(
-        body,
+        plane_body if plane else body,
         mesh=mesh,
         in_specs=placed,
         out_specs=(P(None, "depth", None), P("shot", None, None)),

time: 102 us -> 81.5 us (0.80)
  Pallas kernels: 93.9 us -> 75.2 us
  local copies, waits for them, and re-layouts: 6.52 us -> 5.47 us
    pallas_call x1, Pallas kernels: 93.9 us -> 75.2 us  [plane_body(): pl.pallas_call(functools.partial(plane_kernel, depths), out_shape=(jax.Sh...]
    unnamed x8 -> x5, local copies, waits for them, and re-layouts: 6.52 us -> 5.47 us
where the time goes in v1:
time: 81.5 us; the launch traced here: 81.3 us
  Pallas kernels  75.2 us (92%)
  local copies, waits for them, and re-layouts  5.47 us (7%)
    pallas_call x1, Pallas kernels, plane_body(): pl.pallas_call(functools.partial(plane_kernel, depths), out_shape=(jax.Sh...  75.2 us
    unnamed x5, local copies, waits for them, and re-layouts  5.47 us

profile of v1, /device:TPU:1, one launch (start us, length us, event | category | flops | bytes accessed | tf_op | source)
XLA Modules:
  0.0 81.3 jit_solution(4415192141803349111)
XLA Ops:
  0.6 2.0 %copy.8 = bf16[1,64,32,128]{3,1,2,0:T(8,128)(2,1)} copy(bf16[1,64,32,128]{3,2,1,0:T(8,128)(2,1)} %param.3) | data formatting | bytes 1048576 | tf_op args[0]
  2.7 75.2 %shard_map.50 = (f32[32,64,128]{2,1,0:T(8,128)}, f32[64,64]{1,0:T(8,128)}) custom-call(bf16[32,64,128]{2,1,0:T(8,128)(2,1)} %bitcast.8, f32[32,128]{1,0:T(8,128)} %speed.1, f32[8,64,128]{2,1,0:T(8,128)} %bitcast.10), custom_call_target="tpu_custom_call" | custom-call | tf_op jit(solution)/shard_map/pallas_call | solution.py:860
  77.8 0.0 copy-start
  77.8 2.8 %copy.6 = f32[64,32,128]{2,1,0:T(8,128)} copy(f32[64,32,128]{2,0,1:T(8,128)} %bitcast.9) | data formatting | bytes 2097152
  80.7 0.0 copy-done
  80.7 0.6 copy.10
Async XLA Ops:
  77.8 2.8 %copy-start = (f32[64,64]{1,0:T(8,128)S(1)}, f32[64,64]{1,0:T(8,128)}, u32[]{:S(2)}) copy-start(f32[64,64]{1,0:T(8,128)} %get-tuple-element.5) | copy-start | bytes 49156

commit v2 on v1

--- a/solution.py
+++ b/solution.py
@@ -486,6 +486,11 @@
 
     used = [0]
 
+    def apart(work):
+        @pl.loop(0, 1 + shot // shots)
+        def _(_):
+            work()
+
     def take(count):
         used[0] += count
         return used[0] - count
@@ -614,14 +619,19 @@
     gram = lax.fori_loop(0, rows // WIDTH, gram_body, zero)
 
     def depth_start(source, into, sem):
-        for j in range(1, depths):
-            other = lax.rem(depth + j, depths)
-            copy(source, into.at[depth], sem + j, (shot, other)).start()
+        @apart
+        def _():
+            for j in range(1, depths):
+                other = lax.rem(depth + j, depths)
+                copy(source, into.at[depth], sem + j, (shot, other)).start()
 
     def depth_finish(source, into, sem, value):
-        for j in range(1, depths):
-            other = lax.rem(depth + j, depths)
-            copy(source, into.at[depth], sem + j, (shot, other)).wait_recv()
+        @apart
+        def _():
+            for j in range(1, depths):
+                other = lax.rem(depth + j, depths)
+                copy(source, into.at[depth], sem + j, (shot, other)).wait_recv()
+
         total = None
         for j in range(depths):
             one = jnp.where(depth == j, value, into[j])
@@ -640,15 +650,17 @@
         whole[w, own_rows] = pair[shot * per + w]
     gram_all[mine] = depth_finish(first_sum, first_in, first_sem, half)
     first_pair = copy(gram_all.at[mine], gram_all.at[mine], first_pair_sem, (flip(1), depth))
-    first_pair.start()
-    first_pair.wait_recv()
+    apart(first_pair.start)
+    apart(first_pair.wait_recv)
     gram = gram_all[...]
 
     low = inverse_factor(gram[:rank, :rank])
     high = inverse_factor(gram[rank:, rank:])
 
-    for mask in range(2, shots):
-        spread_copy(flip(mask), mask).wait_recv()
+    @apart
+    def _():
+        for mask in range(2, shots):
+            spread_copy(flip(mask), mask).wait_recv()
 
     def cross(first, second, size):
         total = None
@@ -670,18 +682,27 @@
     def scatter(source, into, sem, mask):
         return copy(source.at[flip(mask)], into.at[mask], sem + mask, (flip(mask), depth))
 
-    for mask in range(1, shots):
-        scatter(quad_part, quad_in, quad_sem, mask).start()
+    @apart
+    def _():
+        for mask in range(1, shots):
+            scatter(quad_part, quad_in, quad_sem, mask).start()
+
     value = cross(0, 4 * rank, 4 * rank)
     for i in range(shots):
         root_part[i] = value[i * tall : (i + 1) * tall]
-    for mask in range(1, shots):
-        scatter(root_part, root_in, root_sem, mask).start()
+    @apart
+    def _():
+        for mask in range(1, shots):
+            scatter(root_part, root_in, root_sem, mask).start()
 
     def scattered(source, into, sem):
+        @apart
+        def _():
+            for mask in range(1, shots):
+                scatter(source, into, sem, mask).wait_recv()
+
         total = source[shot]
         for mask in range(1, shots):
-            scatter(source, into, sem, mask).wait_recv()
             total = total + into[mask]
         return total
 
@@ -705,31 +726,38 @@
     quad_mixer[...] = mine_quad
     exchange_sem = take(2)
     quad_exchange = copy(quad_mixer, quad_mixer_in, exchange_sem, (flip(2), depth))
-    quad_exchange.start()
+    apart(quad_exchange.start)
 
     quad_at = 2 * low_x + core
     quad_all[pl.ds(pl.multiple_of(quad_at * tall, tall), tall)] = depth_finish(
         quad_sum, quad_depth, quad_depth_sem, quad_own
     )
-    for mask in range(1, 4):
-        piece_copy(quad_all, quad_at, quad_all_sem, mask).start()
+    @apart
+    def _():
+        for mask in range(1, 4):
+            piece_copy(quad_all, quad_at, quad_all_sem, mask).start()
+
     root_own = scattered(root_part, root_in, root_sem)
     root_sum[...] = root_own
     depth_start(root_sum, root_depth, root_depth_sem)
-    for mask in range(1, 4):
-        piece_copy(quad_all, quad_at, quad_all_sem, mask).wait_recv()
+    @apart
+    def _():
+        for mask in range(1, 4):
+            piece_copy(quad_all, quad_at, quad_all_sem, mask).wait_recv()
 
     quad = quad_all[...]
     near = choose(low_x, mm(mine_quad, quad), mm(mine_quad, quad, NT))
-    quad_exchange.wait_recv()
+    apart(quad_exchange.wait_recv)
     their_quad = quad_mixer_in[...]
     mixed = merged(sketch, near, their_quad)
 
     root_all[pl.ds(pl.multiple_of(shot * tall, tall), tall)] = depth_finish(
         root_sum, root_depth, root_depth_sem, root_own
     )
-    for mask in range(1, shots):
-        piece_copy(root_all, shot, root_all_sem, mask).start()
+    @apart
+    def _():
+        for mask in range(1, shots):
+            piece_copy(root_all, shot, root_all_sem, mask).start()
 
     inverse = inverse_factor(mixed)
     sketch = sketches[3]
@@ -744,13 +772,16 @@
     mine_root = mm(carry, joined)
     root_mixer[...] = mine_root
     root_exchange = copy(root_mixer, root_mixer_in, exchange_sem + 1, (flip(4), depth))
-    root_exchange.start()
-    for mask in range(1, shots):
-        piece_copy(root_all, shot, root_all_sem, mask).wait_recv()
+    apart(root_exchange.start)
+
+    @apart
+    def _():
+        for mask in range(1, shots):
+            piece_copy(root_all, shot, root_all_sem, mask).wait_recv()
 
     root = root_all[...]
     near = choose(low_y, mm(mine_root, root), mm(mine_root, root, NT))
-    root_exchange.wait_recv()
+    apart(root_exchange.wait_recv)
     their_root = root_mixer_in[...]
     inverse = inverse_factor(merged(sketch, near, their_root))
     mine_root = mm(inverse, mine_root)
@@ -778,8 +809,11 @@
         out = mm3(parts, split(jnp.concatenate([whole[2 * i], whole[2 * i + 1]], axis=1)))
         for w in range(2):
             gathered[shot * per + 2 * i + w] = out[:, w * cells : (w + 1) * cells]
-        for mask in (6, 2, 4, 1):
-            share_copy(mask, i).start()
+
+        @apart
+        def _():
+            for mask in (6, 2, 4, 1):
+                share_copy(mask, i).start()
 
     own = choose(low_x, mine_root[:, : 2 * rank], mine_root[:, 2 * rank :])
     other = choose(low_x, mine_root[:, 2 * rank :], mine_root[:, : 2 * rank])
@@ -789,13 +823,15 @@
     near += choose(low_x, far[:, : 2 * rank], far[:, 2 * rank :])
     cores[...] = choose(core, near[:, :rank], near[:, rank:]) * (1.0 / math.sqrt(rank))
 
-    for i in range(per // 2):
-        for mask in (2, 4, 6):
-            share_copy(mask, i).wait_recv()
-            forward_copy(mask, i).start()
-    for i in range(per // 2):
-        for mask in (1, 3, 5, 7):
-            share_copy(mask, i).wait_recv()
+    @apart
+    def _():
+        for i in range(per // 2):
+            for mask in (2, 4, 6):
+                share_copy(mask, i).wait_recv()
+                forward_copy(mask, i).start()
+        for i in range(per // 2):
+            for mask in (1, 3, 5, 7):
+                share_copy(mask, i).wait_recv()
 
     out_copy = pltpu.make_async_copy(gathered, basis, local_sems.at[0])
     out_copy.start()

time: 81.5 us -> 75.3 us (0.924)
  Pallas kernels: 75.2 us -> 69 us
    pallas_call x1, Pallas kernels: 75.2 us -> 69 us  [plane_body(): pl.pallas_call(functools.partial(plane_kernel, depths), out_shape=(jax.Sh...]
where the time goes in v2:
time: 75.3 us; the launch traced here: 75.1 us
  Pallas kernels  69 us (92%)
  local copies, waits for them, and re-layouts  5.47 us (7%)
    pallas_call x1, Pallas kernels, plane_body(): pl.pallas_call(functools.partial(plane_kernel, depths), out_shape=(jax.Sh...  69 us
    unnamed x5, local copies, waits for them, and re-layouts  5.47 us

profile of v2, /device:TPU:1, one launch (start us, length us, event | category | flops | bytes accessed | tf_op | source)
XLA Modules:
  0.0 75.1 jit_solution(11312422835168684203)
XLA Ops:
  0.6 2.0 %copy.8 = bf16[1,64,32,128]{3,1,2,0:T(8,128)(2,1)} copy(bf16[1,64,32,128]{3,2,1,0:T(8,128)(2,1)} %param.3) | data formatting | bytes 1048576 | tf_op args[0]
  2.7 69.0 %shard_map.50 = (f32[32,64,128]{2,1,0:T(8,128)}, f32[64,64]{1,0:T(8,128)}) custom-call(bf16[32,64,128]{2,1,0:T(8,128)(2,1)} %bitcast.8, f32[32,128]{1,0:T(8,128)} %speed.1, f32[8,64,128]{2,1,0:T(8,128)} %bitcast.10), custom_call_target="tpu_custom_call" | custom-call | tf_op jit(solution)/shard_map/pallas_call | solution.py:896
  71.7 0.0 copy-start
  71.7 2.8 %copy.6 = f32[64,32,128]{2,1,0:T(8,128)} copy(f32[64,32,128]{2,0,1:T(8,128)} %bitcast.9) | data formatting | bytes 2097152
  74.5 0.0 copy-done
  74.5 0.6 copy.10
Async XLA Ops:
  71.7 2.8 %copy-start = (f32[64,64]{1,0:T(8,128)S(1)}, f32[64,64]{1,0:T(8,128)}, u32[]{:S(2)}) copy-start(f32[64,64]{1,0:T(8,128)} %get-tuple-element.5) | copy-start | bytes 49156

commit v3 on v2

--- a/solution.py
+++ b/solution.py
@@ -425,11 +425,16 @@
 
 def plane_kernel(
     depths,
+    probes_in,
+    speed_in,
+    sketches_in,
+    basis,
+    cores,
     probes,
     speed,
     sketches,
-    basis,
-    cores,
+    flat,
+    edges,
     halo,
     wide_speed,
     field_a,
@@ -458,7 +463,7 @@
     recv_sems,
     local_sems,
 ):
-    rows, rank, cells = probes.shape
+    rank, rows, cells = probes.shape
     shots = 8
     per = rows // shots
     part = 2 * rank // 4
@@ -482,7 +487,34 @@
     for j in range(1, depths):
         other = lax.rem(depth + j, depths)
         pl.semaphore_signal(barrier, inc=1, device_id=(shot, other), device_id_type=MESH)
-    pl.semaphore_wait(barrier, shots - 1 + depths - 1)
+
+    loads = [
+        pltpu.make_async_copy(probes_in, probes, local_sems.at[rows]),
+        pltpu.make_async_copy(speed_in, speed, local_sems.at[rows + 1]),
+        pltpu.make_async_copy(sketches_in, sketches, local_sems.at[rows + 2]),
+    ]
+    for c in loads:
+        c.start()
+    loads[0].wait()
+
+    @pl.loop(0, rank, unroll=4)
+    def _(i):
+        at = pl.ds(pl.multiple_of(i * rows, rows), rows)
+        flat[at] = probes[i].astype(jnp.float32)
+
+    @pl.loop(0, rows, unroll=4)
+    def _(d):
+        field_a[STEPS + d] = flat[pl.ds(d, rank, stride=rows)]
+
+    for d in range(STEPS):
+        edges[0, d] = field_a[rows + d].astype(jnp.bfloat16)
+        edges[1, d] = field_a[STEPS + d].astype(jnp.bfloat16)
+    loads[1].wait()
+    wide_speed[STEPS : STEPS + rows] = speed[...]
+
+    @pl.loop(0, 1 + shot // shots)
+    def _(_):
+        pl.semaphore_wait(barrier, shots - 1 + depths - 1)
 
     used = [0]
 
@@ -512,7 +544,7 @@
         rows_out = pl.ds(rows - STEPS, STEPS) if side == 0 else pl.ds(0, STEPS)
         at = 0 if side == 0 else STEPS + rows
         return (
-            copy(probes.at[rows_out], halo.at[side], halo_sem + side, (shot, to)),
+            copy(edges.at[side], halo.at[side], halo_sem + side, (shot, to)),
             copy(
                 speed.at[rows_out],
                 wide_speed.at[pl.ds(at, STEPS)],
@@ -530,12 +562,6 @@
     def _():
         for c in halo_copies(1):
             c.start()
-
-    @pl.loop(0, rows, unroll=4)
-    def _(d):
-        field_a[STEPS + d] = probes[d].astype(jnp.float32)
-
-    wide_speed[STEPS : STEPS + rows] = speed[...]
 
     @pl.when(depth > 0)
     def _():
@@ -654,6 +680,7 @@
     apart(first_pair.wait_recv)
     gram = gram_all[...]
 
+    loads[2].wait()
     low = inverse_factor(gram[:rank, :rank])
     high = inverse_factor(gram[rank:, rank:])
 
@@ -823,18 +850,26 @@
     near += choose(low_x, far[:, : 2 * rank], far[:, 2 * rank :])
     cores[...] = choose(core, near[:, :rank], near[:, rank:]) * (1.0 / math.sqrt(rank))
 
+    def out_copy(row):
+        return pltpu.make_async_copy(gathered.at[row], basis.at[:, row], local_sems.at[row])
+
+    def put(mask, i):
+        for w in range(2):
+            out_copy(flip(mask) * per + 2 * i + w).start()
+
     @apart
     def _():
+        for i in range(per // 2):
+            put(0, i)
         for i in range(per // 2):
             for mask in (2, 4, 6):
                 share_copy(mask, i).wait_recv()
                 forward_copy(mask, i).start()
+                put(mask, i)
         for i in range(per // 2):
             for mask in (1, 3, 5, 7):
                 share_copy(mask, i).wait_recv()
-
-    out_copy = pltpu.make_async_copy(gathered, basis, local_sems.at[0])
-    out_copy.start()
+                put(mask, i)
 
     @pl.when(depth < depths - 1)
     def _():
@@ -872,7 +907,8 @@
             share_copy(mask, i).wait_send()
         for mask in (2, 4, 6):
             forward_copy(mask, i).wait_send()
-    out_copy.wait()
+    for row in range(rows):
+        out_copy(row).wait()
     assert used[0] <= SEMS
 
 
@@ -882,8 +918,8 @@
 def plane_body(probes, courant, sketches):
     depths = lax.axis_size("depth")
     shots = lax.axis_size("shot")
-    local = jnp.transpose(probes[0], (1, 0, 2))
-    rows, rank, cells = local.shape
+    local = probes[0]
+    rank, rows, cells = local.shape
     per = rows // shots
     tall = rank // 2
     f32 = jnp.float32
@@ -896,12 +932,17 @@
     basis, cores = pl.pallas_call(
         functools.partial(plane_kernel, depths),
         out_shape=(
-            jax.ShapeDtypeStruct((rows, rank, cells), f32),
+            jax.ShapeDtypeStruct((rank, rows, cells), f32),
             jax.ShapeDtypeStruct((rank, rank), f32),
         ),
-        in_specs=[vmem] * 3,
+        in_specs=[pl.BlockSpec(memory_space=pl.ANY)] * 3,
         out_specs=(pl.BlockSpec(memory_space=pl.ANY), vmem),
         scratch_shapes=[
+            pltpu.VMEM((rank, rows, cells), jnp.bfloat16),
+            scratch(rows, cells),
+            scratch(shots, rank, 2 * rank),
+            scratch(rank * rows, cells),
+            pltpu.VMEM((2, STEPS, rank, cells), jnp.bfloat16),
             pltpu.VMEM((2, STEPS, rank, cells), jnp.bfloat16),
             scratch(rows + 2 * STEPS, cells),
             scratch(rows + 2 * STEPS, rank, cells),
@@ -928,13 +969,13 @@
             scratch(rows, rank, cells),
             dma((SEMS,)),
             dma((SEMS,)),
-            dma((1,)),
+            dma((rows + 3,)),
         ],
         compiler_params=pltpu.CompilerParams(
             collective_id=0, has_side_effects=True, vmem_limit_bytes=56 * 2**20
         ),
     )(local, courant, jnp.transpose(sketches, (0, 2, 1)))
-    return (jnp.transpose(basis, (1, 0, 2)), cores[None])
+    return (basis, cores[None])
 
 
 def solution(mesh):

time: 75.3 us -> 71.6 us (0.951)
  local copies, waits for them, and re-layouts: 5.47 us -> 2.89 us
  Pallas kernels: 69 us -> 67.9 us
    unnamed x5 -> x4, local copies, waits for them, and re-layouts: 5.47 us -> 2.89 us
    pallas_call x1, Pallas kernels: 69 us -> 67.9 us  [plane_body(): pl.pallas_call(functools.partial(plane_kernel, depths), out_shape=(jax.Sh...]
where the time goes in v3:
time: 71.6 us; the launch traced here: 71.5 us
  Pallas kernels  67.9 us (95%)
  local copies, waits for them, and re-layouts  2.89 us (4%)
    pallas_call x1, Pallas kernels, plane_body(): pl.pallas_call(functools.partial(plane_kernel, depths), out_shape=(jax.Sh...  67.9 us
    unnamed x4, local copies, waits for them, and re-layouts  2.89 us

profile of v3, /device:TPU:1, one launch (start us, length us, event | category | flops | bytes accessed | tf_op | source)
XLA Modules:
  0.0 71.5 jit_solution(14761213413288744414)
XLA Ops:
  0.6 67.9 %shard_map.50 = (f32[64,32,128]{2,1,0:T(8,128)}, f32[64,64]{1,0:T(8,128)}) custom-call(bf16[64,32,128]{2,1,0:T(8,128)(2,1)} %bitcast.3, f32[32,128]{1,0:T(8,128)} %speed_in.1, f32[8,64,128]{2,1,0:T(8,128)} %bitcast.4), custom_call_target="tpu_custom_call" | custom-call | tf_op jit(solution)/shard_map/pallas_call | solution.py:932
  68.6 0.0 copy-start
  68.6 2.3 %copy.7 = f32[64,32,128]{2,1,0:T(8,128)} copy(f32[64,32,128]{2,1,0:T(8,128)} %get-tuple-element.8) | data formatting | bytes 2097152
  70.8 0.0 copy-done
  70.9 0.6 copy.8
Async XLA Ops:
  68.6 2.3 %copy-start = (f32[64,64]{1,0:T(8,128)S(1)}, f32[64,64]{1,0:T(8,128)}, u32[]{:S(2)}) copy-start(f32[64,64]{1,0:T(8,128)} %get-tuple-element.5) | copy-start | bytes 49156

commit v4 on v3

--- a/solution.py
+++ b/solution.py
@@ -46,21 +46,37 @@
     ).astype(jnp.float32)
     a = jnp.concatenate([gram, eye], axis=1)
     blocks = [a[8 * b : 8 * b + 8] for b in range(n // 8)]
-    for k in range(0, n, 2):
-        b0, r = divmod(k, 8)
-        first, second = blocks[b0][r : r + 1], blocks[b0][r + 1 : r + 2]
-        p, q, s = first[:, k : k + 1], second[:, k : k + 1], second[:, k + 1 : k + 2]
-        if k == n - 2:
-            break
-        scale = 1.0 / (p * s - q * q)
-        row0 = (s * first - q * second) * scale
-        row1 = (p * second - q * first) * scale
-        for b in range((k + 2) // 8, n // 8):
-            col0, col1 = blocks[b][:, k : k + 1], blocks[b][:, k + 1 : k + 2]
-            if b == b0:
-                below = rows[:8] > r + 1
-                col0, col1 = jnp.where(below, col0, 0.0), jnp.where(below, col1, 0.0)
-            blocks[b] = blocks[b] - (col0 * row0 + col1 * row1)
+    inner = lax.broadcasted_iota(jnp.int32, (8, 2 * n), 0)
+    for head in range(n // 8):
+        columns = {
+            b: [
+                jnp.broadcast_to(blocks[b][:, 8 * head + j : 8 * head + j + 1], (8, 2 * n))
+                for j in range(8)
+            ]
+            for b in range(head, n // 8)
+        }
+        for k in range(0, 8, 2):
+            if 8 * head + k == n - 2:
+                break
+            top = columns[head]
+            p, q, s = top[k][k : k + 1], top[k][k + 1 : k + 2], top[k + 1][k + 1 : k + 2]
+            scale = 1.0 / (p * s - q * q)
+            p, q, s = p * scale, q * scale, s * scale
+
+            def solved(x):
+                first, second = x[k : k + 1], x[k + 1 : k + 2]
+                return s * first - q * second, p * second - q * first
+
+            pivots = {j: solved(top[j]) for j in range(k + 2, 8)}
+            row0, row1 = solved(blocks[head])
+            for b in range(head if k < 6 else head + 1, n // 8):
+                col0, col1 = columns[b][k], columns[b][k + 1]
+                if b == head:
+                    below = inner > k + 1
+                    col0, col1 = jnp.where(below, col0, 0.0), jnp.where(below, col1, 0.0)
+                for j, (one, two) in pivots.items():
+                    columns[b][j] = columns[b][j] - (col0 * one + col1 * two)
+                blocks[b] = blocks[b] - (col0 * row0 + col1 * row1)
     a = jnp.concatenate(blocks, axis=0)
     before = jnp.concatenate([a[n - 1 :], a[: n - 1]], axis=0)
     even = lax.rem(rows, 2) == 0
@@ -684,6 +700,20 @@
     low = inverse_factor(gram[:rank, :rank])
     high = inverse_factor(gram[rank:, rank:])
 
+    sketch = sketches[shot // 2 * 2]
+    left = mm(sketch[:, :rank], low)
+    right = mm(sketch[:, rank:], high)
+    mixed = merged(sketch, mm(left, gram[:rank, rank:]), right)
+
+    inverse = inverse_factor(mixed)
+    sketch = sketches[shot // 4 * 4 + 1]
+    carry = mm(choose(low_x, sketch[:, :rank], sketch[:, rank:]), inverse)
+    mine_quad = mm(carry, jnp.concatenate([left, right], axis=1))
+    quad_mixer[...] = mine_quad
+    exchange_sem = take(2)
+    quad_exchange = copy(quad_mixer, quad_mixer_in, exchange_sem, (flip(2), depth))
+    apart(quad_exchange.start)
+
     @apart
     def _():
         for mask in range(2, shots):
@@ -737,24 +767,13 @@
         here = pl.ds(pl.multiple_of(at * tall, tall), tall)
         return copy(ref.at[here], ref.at[here], sem + mask, (flip(mask), depth))
 
-    sketch = sketches[shot // 2 * 2]
-    left = mm(sketch[:, :rank], low)
-    right = mm(sketch[:, rank:], high)
-    mixed = merged(sketch, mm(left, gram[:rank, rank:]), right)
-
     quad_own = scattered(quad_part, quad_in, quad_sem)
     quad_sum[...] = quad_own
     depth_start(quad_sum, quad_depth, quad_depth_sem)
 
-    inverse = inverse_factor(mixed)
-    sketch = sketches[shot // 4 * 4 + 1]
-    carry = mm(choose(low_x, sketch[:, :rank], sketch[:, rank:]), inverse)
-    mine_quad = mm(carry, jnp.concatenate([left, right], axis=1))
-    quad_mixer[...] = mine_quad
-    exchange_sem = take(2)
-    quad_exchange = copy(quad_mixer, quad_mixer_in, exchange_sem, (flip(2), depth))
-    apart(quad_exchange.start)
-
+    root_own = scattered(root_part, root_in, root_sem)
+    root_sum[...] = root_own
+    depth_start(root_sum, root_depth, root_depth_sem)
     quad_at = 2 * low_x + core
     quad_all[pl.ds(pl.multiple_of(quad_at * tall, tall), tall)] = depth_finish(
         quad_sum, quad_depth, quad_depth_sem, quad_own
@@ -764,9 +783,6 @@
         for mask in range(1, 4):
             piece_copy(quad_all, quad_at, quad_all_sem, mask).start()
 
-    root_own = scattered(root_part, root_in, root_sem)
-    root_sum[...] = root_own
-    depth_start(root_sum, root_depth, root_depth_sem)
     @apart
     def _():
         for mask in range(1, 4):

time: 71.6 us -> 65.4 us (0.913)
  Pallas kernels: 67.9 us -> 61.7 us
    pallas_call x1, Pallas kernels: 67.9 us -> 61.7 us  [plane_body(): pl.pallas_call(functools.partial(plane_kernel, depths), out_shape=(jax.Sh...]
where the time goes in v4:
time: 65.4 us; the launch traced here: 65.2 us
  Pallas kernels  61.7 us (94%)
  local copies, waits for them, and re-layouts  2.89 us (4%)
    pallas_call x1, Pallas kernels, plane_body(): pl.pallas_call(functools.partial(plane_kernel, depths), out_shape=(jax.Sh...  61.7 us
    unnamed x4, local copies, waits for them, and re-layouts  2.89 us

profile of v4, /device:TPU:1, one launch (start us, length us, event | category | flops | bytes accessed | tf_op | source)
XLA Modules:
  0.0 65.2 jit_solution(15972000049493635531)
XLA Ops:
  0.6 61.7 %shard_map.50 = (f32[64,32,128]{2,1,0:T(8,128)}, f32[64,64]{1,0:T(8,128)}) custom-call(bf16[64,32,128]{2,1,0:T(8,128)(2,1)} %bitcast.3, f32[32,128]{1,0:T(8,128)} %speed_in.1, f32[8,64,128]{2,1,0:T(8,128)} %bitcast.4), custom_call_target="tpu_custom_call" | custom-call | tf_op jit(solution)/shard_map/pallas_call | solution.py:948
  62.3 0.0 copy-start
  62.3 2.3 %copy.7 = f32[64,32,128]{2,1,0:T(8,128)} copy(f32[64,32,128]{2,1,0:T(8,128)} %get-tuple-element.8) | data formatting | bytes 2097152
  64.6 0.0 copy-done
  64.6 0.6 copy.8
Async XLA Ops:
  62.3 2.3 %copy-start = (f32[64,64]{1,0:T(8,128)S(1)}, f32[64,64]{1,0:T(8,128)}, u32[]{:S(2)}) copy-start(f32[64,64]{1,0:T(8,128)} %get-tuple-element.5) | copy-start | bytes 49156
